TPU v7x, 32 devices: a whole 2x2x4 slice. The times are simulated.
32 devices in a mesh: tm: 2 (over x), band: 16 (over z, y, core).
Axes of the slice: x: 2, y: 2, z: 4, core: 2. Of those that a mesh axis runs over, the one named last changes fastest.
Arguments:
- samples: bfloat16 [512, 256, 2, 512], P('tm', 'band'), may hold values from -6 to 6
- weights: bfloat16 [256, 2, 512, 512], P('band', None, None, 'tm'), may hold values from -0.25 to 0.25
- prototype: float32 [1024], replicated, may hold values from 0.25 to 1
Outputs:
- beam_series: float32 [512, 131072], P('band', 'tm')
All inputs are finite; a program needn't handle non-finite values.
Results may differ from a plain program's by a relative error of at most 0.004.
Values may be sent and summed in bfloat16 or wider, within the bound.
A program may use at most 128 MiB of HBM per device.

v0:
```python
import math
import jax
import jax.numpy as jnp
from jax import lax
from jax.sharding import PartitionSpec as P

M = 512
K = 256
FIRST_BIN = 32


def passed_along(block, axis, distance):
    devices = range(lax.axis_size(axis))
    route = [(i - distance, i) for i in devices if i - distance in devices]
    return lax.ppermute(block, axis, route)


def synth_table(prototype):
    length = prototype.shape[0]
    bin_index = jnp.arange(K, dtype=jnp.int32) + FIRST_BIN
    tap_index = jnp.arange(length, dtype=jnp.int32)
    phase_index = bin_index[:, None] * tap_index[None, :] % M
    angles = phase_index.astype(jnp.float32) * (2.0 * math.pi / M)
    scaled = prototype[None, :] / math.sqrt(K)
    window_table = jnp.stack([jnp.cos(angles) * scaled, -jnp.sin(angles) * scaled], axis=1)
    return window_table.astype(jnp.bfloat16)


def intersection_add(frames, hop_size):
    pieces = frames.shape[-1] // hop_size
    pieces_view = frames.reshape(frames.shape[:-1] + (pieces, hop_size))
    leading = [(0, 0)] * (pieces_view.ndim - 3)
    intersection = jnp.zeros(
        pieces_view.shape[:-3] + (pieces_view.shape[-3] + pieces - 1, hop_size), frames.dtype
    )
    for lag in range(pieces):
        intersection = intersection + jnp.pad(
            pieces_view[..., lag, :], leading + [(lag, pieces - 1 - lag), (0, 0)]
        )
    return intersection


def beam_form(samples, weights):
    products = jnp.einsum("fkce,kdeb->bkdcf", samples, weights, preferred_element_type=jnp.float32)
    real_part = products[:, :, 0, 0] + products[:, :, 1, 1]
    imag_part = products[:, :, 0, 1] - products[:, :, 1, 0]
    return jnp.stack([real_part, imag_part], axis=2).astype(jnp.bfloat16)


def synthesize(spectra, window_table):
    return jnp.einsum("bkcf,kcn->bfn", spectra, window_table, preferred_element_type=jnp.float32)


def shards(samples, weights, prototype):
    hop_size = M // 2
    beam_parts = beam_form(samples, lax.all_gather(weights, "tm", axis=3, tiled=True))
    gathered = lax.all_to_all(beam_parts, "band", split_axis=0, concat_axis=1, tiled=True)
    window_table = synth_table(prototype)
    frame_total = gathered.shape[3]
    tail_rows = prototype.shape[0] // hop_size - 1
    frames = synthesize(gathered, window_table)
    summed = intersection_add(frames, hop_size)
    prev_tail = passed_along(summed[:, frame_total:], "tm", 1)
    block_out = summed[:, :frame_total]
    block_out = jnp.concatenate(
        [block_out[:, :tail_rows] + prev_tail, block_out[:, tail_rows:]], axis=1
    )
    return block_out.reshape(block_out.shape[0], frame_total * hop_size)


def solution(mesh):
    in_specs = (P("tm", "band", None, None), P("band", None, None, "tm"), P())
    out_specs = P("band", "tm")
    return jax.shard_map(shards, mesh=mesh, in_specs=in_specs, out_specs=out_specs, check_vma=False)
```

profile of v0, /device:TPU:16, one launch (start us, length us, event | category | flops | bytes accessed | tf_op | source)
XLA Modules:
  0.0 552.4 jit_solution(13992426558295163922)
XLA Ops:
  6.5 0.0 all-gather.2.cloned.1.call-start
  6.5 12.3 %copy.32 = bf16[16,2,512,256]{2,3,1,0:T(8,128)(2,1)} copy(bf16[16,2,512,256]{3,2,1,0:T(8,128)(2,1)} %param.4) | data formatting | bytes 16777216 | tf_op args[1]
  18.8 0.0 all-gather.2.cloned.1.call-update
  18.8 200.1 %all-gather.2.cloned.1.call-done = bf16[16,2,512,512]{2,3,1,0:T(8,128)(2,1)} async-done(((bf16[16,2,512,256]{2,3,1,0:T(8,128)(2,1)}), bf16[16,2,512,512]{2,3,1,0:T(8,128)(2,1)}) %all-gather.2.cloned.1.call-update) | async-done | bytes 16777232 | tf_op jit(solution)/shard_map/all_gather | solution.py:56
  218.9 27.4 %fusion.2 = f32[512,16,2,2,256]{4,0,3,2,1:T(8,128)} fusion(bf16[16,2,512,512]{2,3,1,0:T(8,128)(2,1)} %all-gather.2.cloned.1.call-done, bf16[256,16,2,512,1]{3,2,1,0,4:T(2,128)(2,1)} %bitcast.63), kind=kOutput, calls=%fused_computation.2 | convolution fusion | flops 8589934592 | bytes 58720256 | tf_op jit(solution)/shard_map/fkce,kdeb->bkdcf/dot_general | solution.py:44
  246.3 6.6 %fusion.10 = bf16[512,16,1,256]{3,0,1,2:T(8,128)(2,1)S(1)} fusion(f32[512,16,2,2,256]{4,0,3,2,1:T(8,128)} %fusion.2), kind=kLoop, calls=%fused_computation.21 | loop fusion | flops 4194304 | bytes 20971520 | tf_op jit(solution)/shard_map/sub | solution.py:46
  252.9 8.5 %fusion.9 = bf16[512,16,1,256]{3,0,1,2:T(8,128)(2,1)} fusion(f32[512,16,2,2,256]{4,0,3,2,1:T(8,128)} %fusion.2), kind=kLoop, calls=%fused_computation.20 | loop fusion | flops 4194304 | bytes 20971520 | tf_op jit(solution)/shard_map/add | solution.py:45
  261.4 6.3 %pad_maximum_fusion = bf16[512,16,2,256]{3,0,1,2:T(8,128)(2,1)} fusion(bf16[512,16,1,256]{3,0,1,2:T(8,128)(2,1)S(1)} %fusion.10, bf16[512,16,1,256]{3,0,1,2:T(8,128)(2,1)} %fusion.9), kind=kLoop, calls=%fused_computation.17 | loop fusion | flops 4194304 | bytes 16777216 | tf_op jit(solution)/shard_map/stack | solution.py:47
  267.8 11.4 %copy.36 = bf16[512,16,2,256]{3,1,2,0:T(8,128)(2,1)} copy(bf16[512,16,2,256]{3,0,1,2:T(8,128)(2,1)} %pad_maximum_fusion) | data formatting | bytes 16777216 | tf_op jit(solution)/shard_map/stack | solution.py:47
  279.2 0.0 copy-start.1
  279.2 6.2 %all-to-all-start = ((bf16[512,16,2,256]{3,1,2,0:T(8,128)(2,1)}), bf16[512,16,2,256]{3,1,2,0:T(8,128)(2,1)}, u32[]{:S(2)}, u32[]{:S(2)}) async-start(bf16[512,16,2,256]{3,1,2,0:T(8,128)(2,1)} %copy.36), calls=%async_computation | async-start | bytes 16777216 | tf_op jit(solution)/shard_map/all_to_all | solution.py:57
  285.4 0.0 copy-done.1
  285.4 4.6 multiply_convert_fusion.1
  290.0 0.1 pad_maximum_fusion.2
  290.1 177.8 %all-to-all-done = bf16[512,16,2,256]{3,1,2,0:T(8,128)(2,1)} async-done(((bf16[512,16,2,256]{3,1,2,0:T(8,128)(2,1)}), bf16[512,16,2,256]{3,1,2,0:T(8,128)(2,1)}, u32[]{:S(2)}, u32[]{:S(2)}) %all-to-all-start) | async-done | bytes 8388640 | tf_op jit(solution)/shard_map/all_to_all | solution.py:57
  467.9 8.0 %copy.37 = bf16[32,16,16,2,256]{4,2,1,3,0:T(8,128)(2,1)} copy(bf16[32,16,16,2,256]{4,2,3,0,1:T(8,128)(2,1)} %bitcast.7) | data formatting | bytes 16777216 | tf_op jit(solution)/shard_map/all_to_all | solution.py:57
  475.9 18.7 %convolution_bitcast_fusion = f32[32,256,4,256]{3,1,2,0:T(8,128)} fusion(bf16[32,256,2,256,1]{3,1,2,4,0:T(8,128)(2,1)} %bitcast.64, bf16[4,256,2,256]{3,1,0,2:T(8,128)(2,1)S(1)} %bitcast.65), kind=kOutput, calls=%fused_computation.3 | convolution fusion | flops 8589934592 | bytes 42991616 | tf_op jit(solution)/shard_map/bkcf,kcn->bfn/dot_general | solution.py:51
  494.6 20.8 %slice_bitcast_fusion.3 = (f32[32,256,256]{2,1,0:T(8,128)S(1)}, f32[32,256,256]{2,1,0:T(8,128)}, f32[32,256,256]{2,1,0:T(8,128)}, f32[32,256,256]{2,1,0:T(8,128)}) fusion(f32[32,256,4,256]{3,1,2,0:T(8,128)} %convolution_bitcast_fusion), kind=kLoop, calls=%fused_computation.10 | loop fusion | bytes 67108864 | tf_op jit(solution)/shard_map/squeeze | solution.py:38
  515.4 1.2 pad_add_fusion.3
  516.6 2.5 collective-permute-start
  519.1 13.6 %pad_add_fusion = f32[32,253,256]{2,1,0:T(8,128)} fusion(f32[32,256,256]{2,1,0:T(8,128)} %get-tuple-element.7, f32[32,256,256]{2,1,0:T(8,128)} %get-tuple-element.8, f32[32,256,256]{2,1,0:T(8,128)} %get-tuple-element.6, f32[32,256,256]{2,1,0:T(8,128)S(1)} %get-tuple-element.5), kind=kLoop, calls=%fused_computation.4 | loop fusion | flops 6217728 | bytes 41844736 | tf_op jit(solution)/shard_map/add | solution.py:37
  532.6 0.0 copy-start
  532.6 0.0 collective-permute-done
  532.6 1.3 add_add_fusion
  533.9 2.3 copy-done
  536.2 1.2 pad_maximum_fusion.1
  537.3 8.3 %copy.56 = f32[4,8,256,256]{3,1,2,0:T(8,128)} copy(f32[4,8,256,256]{3,2,1,0:T(8,128)S(1)} %bitcast.62) | data formatting | bytes 16777216
  (2 shorter events, 0.0 us)
Async XLA Ops:
  6.5 212.4 %all-gather.2.cloned.1.call-start = ((), (), s32[]{:S(2)}) async-start(), calls=%async_computation.1 | async-start | bytes 25165824 | tf_op jit(solution)/shard_map/all_gather | solution.py:56
  279.2 6.2 %copy-start.1 = (f32[1024]{0:T(1024)S(1)}, f32[1024]{0:T(1024)}, u32[]{:S(2)}) copy-start(f32[1024]{0:T(1024)} %param.5) | copy-start | bytes 12292
  279.2 188.7 %all-to-all-start = ((bf16[512,16,2,256]{3,1,2,0:T(8,128)(2,1)}), bf16[512,16,2,256]{3,1,2,0:T(8,128)(2,1)}, u32[]{:S(2)}, u32[]{:S(2)}) async-start(bf16[512,16,2,256]{3,1,2,0:T(8,128)(2,1)} %copy.36), calls=%async_computation | async-start | bytes 16777216 | tf_op jit(solution)/shard_map/all_to_all | solution.py:57
  516.6 16.0 %collective-permute-start = (f32[32,3,256]{2,1,0:T(4,128)S(1)}, f32[32,3,256]{2,1,0:T(4,128)S(1)}, u32[]{:S(2)}, u32[]{:S(2)}) collective-permute-start(f32[32,3,256]{2,1,0:T(4,128)S(1)} %pad_add_fusion.3), channel_id=1, source_target_pairs={{0,16},{1,17},{2,18},{3,19},{4,20},{5,21},{6,22},{7,23},{8,24},{9,... | collective-permute-start | bytes 294920 | tf_op jit(solution)/shard_map/ppermute | solution.py:15
  532.6 3.5 copy-start
Sparse Core Ops, SparseCore 0:
  19.0 199.8 all-gather.1
where the time goes:
time: 553 us; the launch traced here: 552 us
  waiting for transfers between devices  378 us (68%)
  local copies, waits for them, and re-layouts  63 us (11%)
  matrix products  46.1 us (8%)
  other arithmetic  43.4 us (8%)
  between operations  13.5 us (2%)
  starting transfers between devices  8.68 us (2%)
    all_gather x1, waiting for transfers between devices, shards(): lax.all_gather(weights, 'tm', axis=3, tiled=True)  200 us
    all_to_all x1, waiting for transfers between devices, shards(): lax.all_to_all(beam_parts, 'band', split_axis=0, concat_axis=1, tiled=True)  178 us
    dot_general x1, matrix products, beam_form(): jnp.einsum('fkce,kdeb->bkdcf', samples, weights, preferred_element_type=j...  27.4 us
    unnamed x6, local copies, waits for them, and re-layouts  22.8 us
    squeeze x1, local copies, waits for them, and re-layouts, intersection_add(): pieces_view[..., lag, :]  20.8 us
    dot_general x1, matrix products, synthesize(): jnp.einsum('bkcf,kcn->bfn', spectra, window_table, preferred_element_type...  18.7 us
    add x1, other arithmetic, intersection_add(): intersection + jnp.pad(pieces_view[..., lag, :], leading + [(lag, pieces...  13.6 us
    another operation x1, local copies, waits for them, and re-layouts, beam_form(): return jnp.stack([real_part, imag_part], axis=2).astype(jnp.bfloat16)  11.4 us
  transfers between devices with their start and end apart: 3, of which 2 were waited for; matrix products, arithmetic and copies ran while one was open for 3% of the time, Pallas kernels for 0%

commit v1 on v0

--- a/solution.py
+++ b/solution.py
@@ -54,7 +54,12 @@
 def shards(samples, weights, prototype):
     hop_size = M // 2
     beam_parts = beam_form(samples, lax.all_gather(weights, "tm", axis=3, tiled=True))
-    gathered = lax.all_to_all(beam_parts, "band", split_axis=0, concat_axis=1, tiled=True)
+    gathered = jnp.concatenate(
+        lax.all_to_all(
+            jnp.stack(jnp.split(beam_parts, lax.axis_size("band"), axis=0)), "band", 0, 0
+        ),
+        axis=1,
+    )
     window_table = synth_table(prototype)
     frame_total = gathered.shape[3]
     tail_rows = prototype.shape[0] // hop_size - 1

time: 553 us -> 550 us (level)
  local copies, waits for them, and re-layouts: 63 us -> 55.1 us
    unnamed x0 -> x15, other arithmetic: none -> 12.4 us
    reshape x0 -> x1, local copies, waits for them, and re-layouts: none -> 11.5 us  [shards(): jnp.concatenate(lax.all_to_all(jnp.stack(jnp.split(beam_parts, lax.axis_s...]
    another operation x1 -> x0, local copies, waits for them, and re-layouts: 11.4 us -> none  [beam_form(): return jnp.stack([real_part, imag_part], axis=2).astype(jnp.bfloat16)]
    all_to_all x1 -> x0, local copies, waits for them, and re-layouts: 8.01 us -> none  [shards(): lax.all_to_all(beam_parts, 'band', split_axis=0, concat_axis=1, tiled=True)]
where the time goes in v1:
time: 550 us; the launch traced here: 549 us
  waiting for transfers between devices  378 us (69%)
  local copies, waits for them, and re-layouts  55.1 us (10%)
  other arithmetic  47.9 us (9%)
  matrix products  46.1 us (8%)
  between operations  13.5 us (2%)
  starting transfers between devices  8.68 us (2%)
    all_gather x1, waiting for transfers between devices, shards(): lax.all_gather(weights, 'tm', axis=3, tiled=True)  200 us
    all_to_all x1, waiting for transfers between devices, shards(): lax.all_to_all(jnp.stack(jnp.split(beam_parts, lax.axis_size('band'), axi...  178 us
    dot_general x1, matrix products, beam_form(): jnp.einsum('fkce,kdeb->bkdcf', samples, weights, preferred_element_type=j...  27.4 us
    unnamed x6, local copies, waits for them, and re-layouts  22.8 us
    squeeze x1, local copies, waits for them, and re-layouts, intersection_add(): pieces_view[..., lag, :]  20.8 us
    dot_general x1, matrix products, synthesize(): jnp.einsum('bkcf,kcn->bfn', spectra, window_table, preferred_element_type...  18.7 us
    add x1, other arithmetic, intersection_add(): intersection + jnp.pad(pieces_view[..., lag, :], leading + [(lag, pieces...  13.3 us
    unnamed x15, other arithmetic  12.4 us
  transfers between devices with their start and end apart: 3, of which 2 were waited for; matrix products, arithmetic and copies ran while one was open for 3% of the time, Pallas kernels for 0%

profile of v1, /device:TPU:16, one launch (start us, length us, event | category | flops | bytes accessed | tf_op | source)
XLA Modules:
  0.0 549.1 jit_solution(10817504798415944509)
XLA Ops:
  6.5 12.3 %copy.11 = bf16[16,2,512,256]{2,3,1,0:T(8,128)(2,1)} copy(bf16[16,2,512,256]{3,2,1,0:T(8,128)(2,1)} %param.4) | data formatting | bytes 16777216 | tf_op args[1]
  18.8 200.1 %all-gather.2.cloned.1.call-done = bf16[16,2,512,512]{2,3,1,0:T(8,128)(2,1)} async-done(((bf16[16,2,512,256]{2,3,1,0:T(8,128)(2,1)}), bf16[16,2,512,512]{2,3,1,0:T(8,128)(2,1)}) %all-gather.2.cloned.1.call-update) | async-done | bytes 16777232 | tf_op jit(solution)/shard_map/all_gather | solution.py:56
  218.9 27.4 %fusion.2 = f32[512,16,2,2,256]{4,0,3,2,1:T(8,128)} fusion(bf16[16,2,512,512]{2,3,1,0:T(8,128)(2,1)} %all-gather.2.cloned.1.call-done, bf16[256,16,2,512,1]{3,2,1,0,4:T(2,128)(2,1)} %bitcast.95), kind=kOutput, calls=%fused_computation.32 | convolution fusion | flops 8589934592 | bytes 58720256 | tf_op jit(solution)/shard_map/fkce,kdeb->bkdcf/dot_general | solution.py:44
  246.3 6.6 %fusion.10 = bf16[512,16,1,256]{3,0,1,2:T(8,128)(2,1)S(1)} fusion(f32[512,16,2,2,256]{4,0,3,2,1:T(8,128)} %fusion.2), kind=kLoop, calls=%fused_computation.50 | loop fusion | flops 4194304 | bytes 20971520 | tf_op jit(solution)/shard_map/sub | solution.py:46
  252.9 6.4 %fusion.9 = bf16[512,16,1,256]{3,0,1,2:T(8,128)(2,1)S(1)} fusion(f32[512,16,2,2,256]{4,0,3,2,1:T(8,128)} %fusion.2), kind=kLoop, calls=%fused_computation.49 | loop fusion | flops 4194304 | bytes 20971520 | tf_op jit(solution)/shard_map/add | solution.py:45
  259.3 0.8 bitcast_dynamic-update-slice_fusion.14
  260.1 0.8 bitcast_dynamic-update-slice_fusion.13
  261.0 0.8 bitcast_dynamic-update-slice_fusion.12
  261.8 0.8 bitcast_dynamic-update-slice_fusion.11
  262.6 0.8 bitcast_dynamic-update-slice_fusion.10
  263.4 0.8 bitcast_dynamic-update-slice_fusion.9
  264.3 0.8 bitcast_dynamic-update-slice_fusion.8
  265.1 0.8 bitcast_dynamic-update-slice_fusion.7
  265.9 0.8 bitcast_dynamic-update-slice_fusion.6
  266.8 0.8 bitcast_dynamic-update-slice_fusion.5
  267.6 0.8 bitcast_dynamic-update-slice_fusion.4
  268.4 0.8 bitcast_dynamic-update-slice_fusion.3
  269.2 0.8 bitcast_dynamic-update-slice_fusion.2
  270.9 0.8 bitcast_dynamic-update-slice_fusion
  272.6 6.2 %all-to-all-start = ((bf16[16,32,16,2,256]{4,1,2,3,0:T(8,128)(2,1)}), bf16[16,32,16,2,256]{4,1,2,3,0:T(8,128)(2,1)}, u32[]{:S(2)}, u32[]{:S(2)}) async-start(bf16[16,32,16,2,256]{4,1,2,3,0:T(8,128)(2,1)} %fusion.35), calls=%async_computation | async-start | bytes 16777216 | tf_op jit(solution)/shard_map/all_to_all | solution.py:58
  278.8 4.6 multiply_convert_fusion.1
  283.5 177.8 %all-to-all-done = bf16[16,32,16,2,256]{4,1,2,3,0:T(8,128)(2,1)} async-done(((bf16[16,32,16,2,256]{4,1,2,3,0:T(8,128)(2,1)}), bf16[16,32,16,2,256]{4,1,2,3,0:T(8,128)(2,1)}, u32[]{:S(2)}, u32[]{:S(2)}) %all-to-all-start) | async-done | bytes 8388640 | tf_op jit(solution)/shard_map/all_to_all | solution.py:58
  461.3 11.5 %copy.15 = bf16[32,16,16,2,256]{4,2,1,3,0:T(8,128)(2,1)} copy(bf16[32,16,16,2,256]{4,0,2,3,1:T(8,128)(2,1)} %bitcast.22) | data formatting | bytes 16777216 | tf_op jit(solution)/shard_map/reshape | solution.py:57
  472.8 18.7 %convolution_bitcast_fusion = f32[32,256,4,256]{3,1,2,0:T(8,128)} fusion(bf16[32,256,2,256,1]{3,1,2,4,0:T(8,128)(2,1)} %bitcast.96, bf16[4,256,2,256]{3,1,0,2:T(8,128)(2,1)S(1)} %bitcast.97), kind=kOutput, calls=%fused_computation.33 | convolution fusion | flops 8589934592 | bytes 42991616 | tf_op jit(solution)/shard_map/bkcf,kcn->bfn/dot_general | solution.py:51
  491.5 20.8 %slice_bitcast_fusion.3 = (f32[32,256,256]{2,1,0:T(8,128)S(1)}, f32[32,256,256]{2,1,0:T(8,128)}, f32[32,256,256]{2,1,0:T(8,128)}, f32[32,256,256]{2,1,0:T(8,128)}) fusion(f32[32,256,4,256]{3,1,2,0:T(8,128)} %convolution_bitcast_fusion), kind=kLoop, calls=%fused_computation.40 | loop fusion | bytes 67108864 | tf_op jit(solution)/shard_map/squeeze | solution.py:38
  512.3 1.2 pad_add_fusion.3
  513.5 2.5 collective-permute-start
  516.0 13.3 %pad_add_fusion = f32[32,253,256]{2,1,0:T(8,128)} fusion(f32[32,256,256]{2,1,0:T(8,128)} %get-tuple-element.7, f32[32,256,256]{2,1,0:T(8,128)} %get-tuple-element.8, f32[32,256,256]{2,1,0:T(8,128)} %get-tuple-element.6, f32[32,256,256]{2,1,0:T(8,128)S(1)} %get-tuple-element.5), kind=kLoop, calls=%fused_computation.34 | loop fusion | flops 6217728 | bytes 41844736 | tf_op jit(solution)/shard_map/add | solution.py:37
  529.3 1.3 add_add_fusion
  530.6 2.3 copy-done
  532.8 1.2 pad_maximum_fusion
  534.0 8.3 %copy.34 = f32[4,8,256,256]{3,1,2,0:T(8,128)} copy(f32[4,8,256,256]{3,2,1,0:T(8,128)S(1)} %bitcast.94) | data formatting | bytes 16777216
  (11 shorter events, 1.8 us)
Async XLA Ops:
  6.5 212.4 %all-gather.2.cloned.1.call-start = ((), (), s32[]{:S(2)}) async-start(), calls=%async_computation.1 | async-start | bytes 25165824 | tf_op jit(solution)/shard_map/all_gather | solution.py:56
  272.5 6.2 %copy-start.1 = (f32[1024]{0:T(1024)S(1)}, f32[1024]{0:T(1024)}, u32[]{:S(2)}) copy-start(f32[1024]{0:T(1024)} %param.5) | copy-start | bytes 12292
  272.6 188.7 %all-to-all-start = ((bf16[16,32,16,2,256]{4,1,2,3,0:T(8,128)(2,1)}), bf16[16,32,16,2,256]{4,1,2,3,0:T(8,128)(2,1)}, u32[]{:S(2)}, u32[]{:S(2)}) async-start(bf16[16,32,16,2,256]{4,1,2,3,0:T(8,128)(2,1)} %fusion.35), calls=%async_computation | async-start | bytes 16777216 | tf_op jit(solution)/shard_map/all_to_all | solution.py:58
  513.5 15.8 %collective-permute-start = (f32[32,3,256]{2,1,0:T(4,128)S(1)}, f32[32,3,256]{2,1,0:T(4,128)S(1)}, u32[]{:S(2)}, u32[]{:S(2)}) collective-permute-start(f32[32,3,256]{2,1,0:T(4,128)S(1)} %pad_add_fusion.3), channel_id=1, source_target_pairs={{0,16},{1,17},{2,18},{3,19},{4,20},{5,21},{6,22},{7,23},{8,24},{9,... | collective-permute-start | bytes 294920 | tf_op jit(solution)/shard_map/ppermute | solution.py:15
  529.3 3.5 copy-start
Sparse Core Ops, SparseCore 0:
  19.0 199.8 all-gather.1
